TPU v7x, 128 devices: a whole 4x4x4 slice. The times are simulated.
128 devices in a mesh: group: 8 (over z, core), pair: 16 (over y, x).
Axes of the slice: x: 4, y: 4, z: 4, core: 2. Of those that a mesh axis runs over, the one named last changes fastest.
Arguments:
- query_embed: bfloat16 [8, 16, 1024], P('group'), may hold values from -6 to 6
- teacher_scores: float32 [8, 16, 16, 32], P('group', 'pair'), may hold values from -9 to 9
- pair_owner: int32 [8, 16, 16, 32, 1], P('group', 'pair'), may hold values from 0 to 127; in each aligned block of 512 rows (0 to 511, 512 to 1023, ..., all dimensions but the last counted through in order) at most 8 rows name the same one
- pair_row: int32 [8, 16, 16, 32], P('group', 'pair'), may hold values from 0 to 2047
- passage_hidden: bfloat16 [262144, 1024], P(('group', 'pair')), may hold values from -24 to 24
- projection: bfloat16 [1024, 1024], replicated, may hold values from -0.1875 to 0.1875
Outputs:
- query_loss: float32 [8, 16], P('group', 'pair')
- query_grad: float32 [8, 16, 1024], P('group', 'pair')
- hidden_grad: bfloat16 [262144, 1024], P(('group', 'pair'))
- projection_grad: float32 [1024, 1024], P(('group', 'pair'))
Inputs may be any that keep to these rules, and one draw needn't show every extreme that they name: `pair_owner`: owners are numbered with group as the slower index. Among the 512 candidates held by one device, at most 8 name the same owner, and every draw has a device and an owner with exactly 8. `pair_row`: A passage may be named by several candidates.
All inputs are finite; a program needn't handle non-finite values.
Results may differ from a plain program's by a relative error of at most 0.022.
Values may be sent and summed in bfloat16 or wider, within the bound.
A program may use at most 128 MiB of HBM per device.

v0:
```python
import math
import jax
import jax.numpy as jnp
from jax import lax
from jax.sharding import PartitionSpec as P

loss_scale = 1024.0
f32, bf16, i32 = (jnp.float32, jnp.bfloat16, jnp.int32)


def iota(shape, dim):
    return lax.broadcasted_iota(i32, shape, dim)


def dot(a, b, ca, cb):
    return lax.dot_general(a, b, (((ca,), (cb,)), ((), ())), preferred_element_type=f32)


def halves(x):
    high = x.astype(bf16)
    return (high, (x - high.astype(f32)).astype(bf16))


def shards(query_embed, teacher_scores, pair_owner, pair_row, passage_hidden, projection):
    width = query_embed.shape[2]
    q_rows = query_embed.shape[1]
    cand = teacher_scores.shape[3]
    n_pair, n_group = (lax.axis_size("pair"), lax.axis_size("group"))
    n_dev = n_pair * n_group
    cap = max(2, 2 * q_rows * cand // n_dev)
    slots = n_pair * cap
    k_all = cand * n_pair
    queries_n = n_group * q_rows
    rows = passage_hidden.shape[0]
    den = float(k_all * (k_all * k_all - 1))
    inv_root = 1.0 / math.sqrt(width)
    r = lax.axis_index("pair")
    owner = pair_owner.reshape(1, q_rows * cand)
    row = pair_row.reshape(1, q_rows * cand)
    n_own = q_rows * cand
    lane = iota((1, n_own), 1)
    owner_hot = iota((n_dev, n_own), 0) == owner
    owner_b = owner_hot.astype(bf16)
    before = (iota((n_own, n_own), 0) < iota((n_own, n_own), 1)).astype(bf16)
    seen = dot(owner_b, before, 1, 0)
    slot = jnp.sum(jnp.where(owner_hot, seen, 0.0), axis=0, keepdims=True).astype(i32)
    at_slot = iota((slots, n_own), 0) == slot + r * cap
    high = (row >> 4) + 1
    low = (row & 15) * 16 + lane // cand
    req = dot(owner_b, jnp.where(at_slot, high, 0).astype(bf16), 1, 1) * 256.0 + dot(
        owner_b, jnp.where(at_slot, low, 0).astype(bf16), 1, 1
    )
    q_all = lax.all_gather(query_embed[0], "group", axis=0, tiled=True)
    got = lax.all_to_all(req, ("group", "pair"), split_axis=0, concat_axis=0, tiled=True)
    packed = got.reshape(n_group, n_pair, slots).sum(1).reshape(1, n_group * slots).astype(i32)
    pq = dot(q_all, projection, 1, 1).astype(bf16)
    s_t = dot(pq, passage_hidden, 1, 1) * inv_root
    s_hi, s_lo = halves(s_t)
    place = (iota((rows, n_group * slots), 0) == (packed >> 4) - 16).astype(bf16)
    z = dot(s_hi, place, 1, 0) + dot(s_lo, place, 1, 0)
    slot_query = (packed & 15) + q_rows * (iota((1, n_group * slots), 1) // slots)
    slot_score = jnp.sum(
        jnp.where(iota((queries_n, n_group * slots), 0) == slot_query, z, 0.0), axis=0
    ).reshape(n_group, 1, slots)
    to_send = jnp.broadcast_to(slot_score, (n_group, n_pair, slots)).reshape(n_dev, slots)
    table = lax.all_to_all(to_send, ("group", "pair"), split_axis=0, concat_axis=0, tiled=True)
    tags = (owner * cap + slot).reshape(q_rows, cand)
    tags_k = lax.all_to_all(tags, "pair", split_axis=0, concat_axis=0, tiled=True).reshape(1, k_all)
    teach_k = lax.all_to_all(
        teacher_scores.reshape(q_rows, cand), "pair", split_axis=0, concat_axis=0, tiled=True
    ).reshape(1, k_all)
    k_owner = (iota((n_dev, k_all), 0) == tags_k // cap).astype(bf16)
    k_slot = (iota((slots, k_all), 0) == tags_k % cap + cap * (iota((1, k_all), 1) // cand)).astype(
        f32
    )
    t_hi, t_lo = halves(table.T)
    picked = dot(t_hi, k_owner, 1, 0) + dot(t_lo, k_owner, 1, 0)
    s_k = jnp.sum(picked * k_slot, axis=0, keepdims=True)
    tanh_s = jnp.tanh(s_k.T - s_k)
    tanh_t = jnp.tanh(teach_k.T - teach_k)
    gap = 0.5 * (jnp.sum(tanh_s, 0, keepdims=True) - jnp.sum(tanh_t, 0, keepdims=True))
    loss = 6.0 * jnp.sum(gap * gap, axis=1, keepdims=True) / den
    grad = loss_scale * 12.0 * gap / den
    s_grad = 0.5 * jnp.sum((grad.T - grad) * (1.0 - tanh_s * tanh_s), axis=0, keepdims=True)
    values = dot(k_owner, (k_slot * s_grad).astype(bf16), 1, 1)
    back = lax.all_to_all(values, ("group", "pair"), split_axis=0, concat_axis=0, tiled=True)
    same_group = (
        iota((queries_n, n_group * slots), 0) // q_rows
        == iota((queries_n, n_group * slots), 1) // slots
    )
    spread = jnp.where(same_group, jnp.tile(back, (1, n_group)), 0.0).astype(bf16)
    w_t = dot(place, spread, 1, 1).astype(bf16)
    hidden_grad = (dot(w_t, pq, 1, 0) * inv_root).astype(bf16)
    u_part = dot(w_t, passage_hidden, 0, 0).astype(bf16)
    u_rows = lax.all_to_all(u_part, ("group", "pair"), split_axis=0, concat_axis=0, tiled=True)
    u_cols = lax.all_to_all(u_part.T, ("group", "pair"), split_axis=0, concat_axis=0, tiled=True)
    u_row = jnp.sum(u_rows.astype(f32), 0, keepdims=True) * inv_root
    u_col = jnp.sum(u_cols.astype(f32).reshape(n_dev, width // n_dev, queries_n), 0) * inv_root
    r_hi, r_lo = halves(u_row)
    c_hi, c_lo = halves(u_col)
    query_grad = dot(r_hi, projection, 1, 0) + dot(r_lo, projection, 1, 0)
    projection_grad = dot(c_hi, q_all, 1, 0) + dot(c_lo, q_all, 1, 0)
    return (loss, query_grad.reshape(1, 1, width), hidden_grad, projection_grad)


def solution(mesh):
    placed = (
        P("group", None, None),
        P("group", "pair", None, None),
        P("group", "pair", None, None, None),
        P("group", "pair", None, None),
        P(("group", "pair"), None),
        P(),
    )
    return jax.shard_map(
        shards,
        mesh=mesh,
        in_specs=placed,
        out_specs=(
            P("group", "pair"),
            P("group", "pair", None),
            P(("group", "pair"), None),
            P(("group", "pair"), None),
        ),
        check_vma=False,
    )
```

profile of v0, /device:TPU:1, one launch (start us, length us, event | category | flops | bytes accessed | tf_op | source)
XLA Modules:
  0.0 141.7 jit_solution(1238981770986733830)
XLA Ops:
  0.6 0.0 copy-start
  0.6 0.8 broadcast_multiply_fusion
  1.5 0.5 broadcast.374
  2.0 1.4 reduce.11
  3.4 0.1 eq.55
  3.5 0.3 fusion.12
  3.7 0.1 convert_element_type.121
  3.8 0.6 add.119
  4.4 7.6 %all-to-all-start = ((s32[16,1,32]{2,1,0:T(1,128)}), s32[16,1,32]{2,1,0:T(1,128)S(1)}, u32[]{:S(2)}, u32[]{:S(2)}) async-start(s32[16,1,32]{2,1,0:T(1,128)} %add.119), calls=%async_computation | async-start | bytes 16384 | tf_op jit(solution)/shard_map/all_to_all | solution.py:68
  12.0 0.7 and_multiply_fusion
  12.7 0.1 mul.135
  12.8 0.1 add.125
  12.9 15.0 %all-gather = bf16[1,128,1024]{2,1,0:T(8,128)(2,1)S(1)} all-gather(bf16[1,16,1024]{2,1,0:T(8,128)(2,1)} %param.6), channel_id=2, replica_groups=mesh['group'=8,'pair'=16] {'group'}, dimensions={1}, use_global_device_ids=true | all-gather | bytes 294912 | tf_op jit(solution)/shard_map/all_gather | solution.py:53
  27.9 0.2 convolution_multiply_fusion.1
  28.1 0.8 convolution_add_fusion.1
  28.9 0.0 copy-done
  28.9 0.8 convolution_convert_fusion
  29.8 4.7 %convolution_multiply_fusion = f32[128,2048]{1,0:T(8,128)} fusion(bf16[128,1024]{1,0:T(8,128)(2,1)S(1)} %convolution_convert_fusion, bf16[2048,1024]{1,0:T(8,128)(2,1)} %param.10), kind=kOutput, calls=%fused_computation.8 | convolution fusion | flops 537133056 | bytes 5505024 | tf_op jit(solution)/shard_map/dot_general | solution.py:16
  34.5 0.0 all-to-all-done
  34.5 6.9 %all-to-all-start.3 = ((f32[16,1,32]{2,1,0:T(1,128)}), f32[16,1,32]{2,1,0:T(1,128)S(1)}, u32[]{:S(2)}, u32[]{:S(2)}) async-start(f32[16,1,32]{2,1,0:T(1,128)} %bitcast.13), calls=%async_computation.3 | async-start | bytes 16384 | tf_op jit(solution)/shard_map/all_to_all | solution.py:69
  41.4 0.7 reduce.12
  42.1 0.1 reshape.365
  42.2 5.6 %all-to-all-done.3 = f32[16,1,32]{2,1,0:T(1,128)S(1)} async-done(((f32[16,1,32]{2,1,0:T(1,128)}), f32[16,1,32]{2,1,0:T(1,128)S(1)}, u32[]{:S(2)}, u32[]{:S(2)}) %all-to-all-start.3) | async-done | bytes 2080 | tf_op jit(solution)/shard_map/all_to_all | solution.py:69
  47.7 6.5 %all-to-all-start.1 = ((f32[128,1,128]{2,1,0:T(1,128)}), f32[128,1,128]{2,1,0:T(1,128)S(1)}, u32[]{:S(2)}, u32[]{:S(2)}) async-start(f32[128,1,128]{2,1,0:T(1,128)} %bitcast.3), calls=%async_computation.1 | async-start | bytes 131072 | tf_op jit(solution)/shard_map/all_to_all | solution.py:54
  54.3 0.5 broadcast.376
  54.8 0.7 reduce.13
  55.5 0.1 sub.123
  55.6 8.3 %all-to-all-done.1 = f32[128,1,128]{2,1,0:T(1,128)S(1)} async-done(((f32[128,1,128]{2,1,0:T(1,128)}), f32[128,1,128]{2,1,0:T(1,128)S(1)}, u32[]{:S(2)}, u32[]{:S(2)}) %all-to-all-start.1) | async-done | bytes 65568 | tf_op jit(solution)/shard_map/all_to_all | solution.py:54
  63.9 0.0 copy-start.2
  63.9 3.3 %fusion.1 = f32[128,1024]{1,0:T(8,128)S(1)} fusion(s32[1024]{0:T(1024)S(1)} %add_bitcast_fusion, f32[128,2048]{1,0:T(8,128)} %convolution_multiply_fusion), kind=kOutput, calls=%fused_computation.3 | convolution fusion | flops 540016640 | bytes 1576960 | tf_op jit(solution)/shard_map/dot_general | solution.py:16
  67.3 0.0 copy-done.2
  67.3 1.8 %fusion.9 = f32[1024]{0:T(1024)S(1)} fusion(f32[128,1024]{1,0:T(8,128)S(1)} %fusion.1, s32[1024]{0:T(1024)S(1)} %add_bitcast_fusion, f32[128,2048]{1,0:T(8,128)S(1)} %copy-done.2, s32[1024]{0:T(1024)S(1)} %bitcast_add_fusion), kind=kOutput, calls=%fused_computation.15 | convolution fusion | flops 539753472 | bytes 1585152 | tf_op jit(solution)/shard_map/dot_general | solution.py:16
  69.1 0.6 broadcast_in_dim.47
  69.7 4.5 %all-to-all-start.2 = ((f32[128,1,128]{2,1,0:T(1,128)}), f32[128,1,128]{2,1,0:T(1,128)S(1)}, u32[]{:S(2)}, u32[]{:S(2)}) async-start(f32[128,1,128]{2,1,0:T(1,128)} %bitcast.9), calls=%async_computation.2 | async-start | bytes 131072 | tf_op jit(solution)/shard_map/all_to_all | solution.py:66
  74.2 0.2 tanh_reduce_fusion
  74.4 9.3 %all-to-all-done.2 = f32[128,1,128]{2,1,0:T(1,128)S(1)} async-done(((f32[128,1,128]{2,1,0:T(1,128)}), f32[128,1,128]{2,1,0:T(1,128)S(1)}, u32[]{:S(2)}, u32[]{:S(2)}) %all-to-all-start.2) | async-done | bytes 65568 | tf_op jit(solution)/shard_map/all_to_all | solution.py:66
  83.7 0.2 fusion.25
  83.9 0.2 fusion.11
  84.1 0.2 fusion.13
  84.4 0.6 broadcast_multiply_fusion.1
  85.0 0.3 multiply_reduce_fusion
  85.3 0.8 fusion.24
  86.1 4.5 %all-to-all-start.4 = ((f32[128,1,128]{2,1,0:T(1,128)}), f32[128,1,128]{2,1,0:T(1,128)S(1)}, u32[]{:S(2)}, u32[]{:S(2)}) async-start(f32[128,1,128]{2,1,0:T(1,128)} %bitcast.16), calls=%async_computation.4 | async-start | bytes 131072 | tf_op jit(solution)/shard_map/all_to_all | solution.py:86
  91.3 8.9 %all-to-all-done.4 = f32[128,1,128]{2,1,0:T(1,128)S(1)} async-done(((f32[128,1,128]{2,1,0:T(1,128)}), f32[128,1,128]{2,1,0:T(1,128)S(1)}, u32[]{:S(2)}, u32[]{:S(2)}) %all-to-all-start.4) | async-done | bytes 65568 | tf_op jit(solution)/shard_map/all_to_all | solution.py:86
  100.2 1.6 %fusion.6 = bf16[2048,128]{1,0:T(8,128)(2,1)S(1)} fusion(s32[1024]{0:T(1024)S(1)} %add_bitcast_fusion, bf16[16,8,8,128]{3,2,1,0:T(8,128)(2,1)S(1)} %bitcast.62, s32[1024]{0:T(1024)S(1)} %get-tuple-element.14, s32[1024]{0:T(1024)S(1)} %get-tuple-element.15, s32[128]{0:T(128)S(1)} %get-tuple-element.16, s32[128]{0:T(128)S(1)} %get-tuple-element.17, ...), kind=kOutput, calls=%fused_computation.9 | convolution fusion | flops 539754496 | bytes 800896 | tf_op jit(solution)/shard_map/dot_general | solution.py:16
  101.8 0.5 copy-done.1
  102.3 0.8 convolution_convert_fusion.1
  103.1 0.5 broadcast.377
  103.6 1.5 %reduce.14 = bf16[128,1024]{1,0:T(8,128)(2,1)} reduce(bf16[128,1,1024]{2,0,1:T(8,128)(2,1)S(1)} %bitcast.58, bf16[]{:T(256)} %broadcast.377), dimensions={1}, to_apply=%copy.19.reduce_sub_computation | reduce | bytes 524290 | tf_op jit(solution)/shard_map/all_to_all | solution.py:95
  105.1 1.8 %reshape.398 = bf16[128,2,512]{2,1,0:T(2,128)(2,1)} reshape(bf16[128,1024]{1,0:T(8,128)(2,1)} %reduce.14) | data formatting | bytes 524288
  106.9 5.4 %all-to-all-start.5 = ((bf16[128,2,512]{2,1,0:T(2,128)(2,1)}), bf16[128,2,512]{2,1,0:T(2,128)(2,1)}, u32[]{:S(2)}, u32[]{:S(2)}) async-start(bf16[128,2,512]{2,1,0:T(2,128)(2,1)} %reshape.398), calls=%async_computation.5 | async-start | bytes 524288 | tf_op jit(solution)/shard_map/all_to_all | solution.py:95
  112.3 0.8 copy.20
  113.2 3.3 %multiply_convert_fusion = bf16[2048,1024]{1,0:T(8,128)(2,1)} fusion(bf16[2048,128]{1,0:T(8,128)(2,1)S(1)} %fusion.6, bf16[128,1024]{1,0:T(8,128)(2,1)S(1)} %convolution_convert_fusion), kind=kOutput, calls=%fused_computation | convolution fusion | flops 541065216 | bytes 4980736 | tf_op jit(solution)/shard_map/dot_general | solution.py:16
  116.4 7.0 %all-to-all-done.5 = bf16[128,2,512]{2,1,0:T(2,128)(2,1)} async-done(((bf16[128,2,512]{2,1,0:T(2,128)(2,1)}), bf16[128,2,512]{2,1,0:T(2,128)(2,1)}, u32[]{:S(2)}, u32[]{:S(2)}) %all-to-all-start.5) | async-done | bytes 262176 | tf_op jit(solution)/shard_map/all_to_all | solution.py:95
  123.4 4.2 %all-to-all-start.6 = ((bf16[128,8,128]{2,1,0:T(8,128)(2,1)}), bf16[128,8,128]{2,1,0:T(8,128)(2,1)S(1)}, u32[]{:S(2)}, u32[]{:S(2)}) async-start(bf16[128,8,128]{2,1,0:T(8,128)(2,1)} %bitcast.23), calls=%async_computation.6 | async-start | bytes 524288 | tf_op jit(solution)/shard_map/all_to_all | solution.py:96
  127.6 2.2 %reshape.399 = bf16[128,1,1024]{2,1,0:T(2,128)(2,1)S(1)} reshape(bf16[128,2,512]{2,1,0:T(2,128)(2,1)} %all-to-all-done.5) | data formatting | bytes 524288
  129.8 0.5 convert_reduce_fusion.1
  130.3 0.4 fusion.68
  130.6 0.4 fusion.67
  131.0 7.9 %all-to-all-done.6 = bf16[128,8,128]{2,1,0:T(8,128)(2,1)S(1)} async-done(((bf16[128,8,128]{2,1,0:T(8,128)(2,1)}), bf16[128,8,128]{2,1,0:T(8,128)(2,1)S(1)}, u32[]{:S(2)}, u32[]{:S(2)}) %all-to-all-start.6) | async-done | bytes 262176 | tf_op jit(solution)/shard_map/all_to_all | solution.py:96
  138.9 0.1 convert_reduce_fusion
  139.0 0.1 fusion.17
  139.2 0.8 convolution_add_fusion.2
  140.0 0.6 add.131
  (16 shorter events, 0.1 us)
Async XLA Ops:
  0.6 28.3 %copy-start = (bf16[1024,1024]{1,0:T(8,128)(2,1)S(1)}, bf16[1024,1024]{1,0:T(8,128)(2,1)}, u32[]{:S(2)}) copy-start(bf16[1024,1024]{1,0:T(8,128)(2,1)} %param.11) | copy-start | bytes 6291460
  4.4 30.0 %all-to-all-start = ((s32[16,1,32]{2,1,0:T(1,128)}), s32[16,1,32]{2,1,0:T(1,128)S(1)}, u32[]{:S(2)}, u32[]{:S(2)}) async-start(s32[16,1,32]{2,1,0:T(1,128)} %add.119), calls=%async_computation | async-start | bytes 16384 | tf_op jit(solution)/shard_map/all_to_all | solution.py:68
  34.5 13.3 %all-to-all-start.3 = ((f32[16,1,32]{2,1,0:T(1,128)}), f32[16,1,32]{2,1,0:T(1,128)S(1)}, u32[]{:S(2)}, u32[]{:S(2)}) async-start(f32[16,1,32]{2,1,0:T(1,128)} %bitcast.13), calls=%async_computation.3 | async-start | bytes 16384 | tf_op jit(solution)/shard_map/all_to_all | solution.py:69
  47.7 16.1 %all-to-all-start.1 = ((f32[128,1,128]{2,1,0:T(1,128)}), f32[128,1,128]{2,1,0:T(1,128)S(1)}, u32[]{:S(2)}, u32[]{:S(2)}) async-start(f32[128,1,128]{2,1,0:T(1,128)} %bitcast.3), calls=%async_computation.1 | async-start | bytes 131072 | tf_op jit(solution)/shard_map/all_to_all | solution.py:54
  63.9 3.4 %copy-start.2 = (f32[128,2048]{1,0:T(8,128)S(1)}, f32[128,2048]{1,0:T(8,128)}, u32[]{:S(2)}) copy-start(f32[128,2048]{1,0:T(8,128)} %convolution_multiply_fusion) | copy-start | bytes 3145732
  69.7 14.0 %all-to-all-start.2 = ((f32[128,1,128]{2,1,0:T(1,128)}), f32[128,1,128]{2,1,0:T(1,128)S(1)}, u32[]{:S(2)}, u32[]{:S(2)}) async-start(f32[128,1,128]{2,1,0:T(1,128)} %bitcast.9), calls=%async_computation.2 | async-start | bytes 131072 | tf_op jit(solution)/shard_map/all_to_all | solution.py:66
  86.1 14.0 %all-to-all-start.4 = ((f32[128,1,128]{2,1,0:T(1,128)}), f32[128,1,128]{2,1,0:T(1,128)S(1)}, u32[]{:S(2)}, u32[]{:S(2)}) async-start(f32[128,1,128]{2,1,0:T(1,128)} %bitcast.16), calls=%async_computation.4 | async-start | bytes 131072 | tf_op jit(solution)/shard_map/all_to_all | solution.py:86
  100.2 2.2 %copy-start.1 = (bf16[2048,1024]{1,0:T(8,128)(2,1)S(1)}, bf16[2048,1024]{1,0:T(8,128)(2,1)}, u32[]{:S(2)}) copy-start(bf16[2048,1024]{1,0:T(8,128)(2,1)} %param.10) | copy-start | bytes 12582916
  106.9 16.5 %all-to-all-start.5 = ((bf16[128,2,512]{2,1,0:T(2,128)(2,1)}), bf16[128,2,512]{2,1,0:T(2,128)(2,1)}, u32[]{:S(2)}, u32[]{:S(2)}) async-start(bf16[128,2,512]{2,1,0:T(2,128)(2,1)} %reshape.398), calls=%async_computation.5 | async-start | bytes 524288 | tf_op jit(solution)/shard_map/all_to_all | solution.py:95
  123.4 15.5 %all-to-all-start.6 = ((bf16[128,8,128]{2,1,0:T(8,128)(2,1)}), bf16[128,8,128]{2,1,0:T(8,128)(2,1)S(1)}, u32[]{:S(2)}, u32[]{:S(2)}) async-start(bf16[128,8,128]{2,1,0:T(8,128)(2,1)} %bitcast.23), calls=%async_computation.6 | async-start | bytes 524288 | tf_op jit(solution)/shard_map/all_to_all | solution.py:96
where the time goes:
time: 142 us
  waiting for transfers between devices  46.8 us (33%)
  starting transfers between devices  39.6 us (28%)
  matrix products  20.5 us (14%)
  blocking collectives  15 us (11%)
  other arithmetic  9 us (6%)
  local copies, waits for them, and re-layouts  8.09 us (6%)
  between operations  2.65 us (2%)
    dot_general x17, matrix products, dot(): lax.dot_general(a, b, (((ca,), (cb,)), ((), ())), preferred_element_type=...  20.5 us
    all_gather x1, blocking collectives, shards(): q_all = lax.all_gather(query_embed[0], 'group', axis=0, tiled=True)  15 us
    all_to_all x1, waiting for transfers between devices, shards(): lax.all_to_all(to_send, ('group', 'pair'), split_axis=0, concat_axis=0, t...  9.29 us
    all_to_all x1, waiting for transfers between devices, shards(): lax.all_to_all(values, ('group', 'pair'), split_axis=0, concat_axis=0, ti...  8.86 us
    all_to_all x1, waiting for transfers between devices, shards(): lax.all_to_all(req, ('group', 'pair'), split_axis=0, concat_axis=0, tiled...  8.3 us
    all_to_all x1, waiting for transfers between devices, shards(): lax.all_to_all(u_part.T, ('group', 'pair'), split_axis=0, concat_axis=0,...  7.87 us
    all_to_all x1, starting transfers between devices, shards(): lax.all_to_all(tags, 'pair', split_axis=0, concat_axis=0, tiled=True)  7.58 us
    all_to_all x1, waiting for transfers between devices, shards(): lax.all_to_all(u_part, ('group', 'pair'), split_axis=0, concat_axis=0, ti...  6.95 us
  transfers between devices with their start and end apart: 7, of which 6 were waited for; matrix products, arithmetic and copies ran while one was open for 12% of the time, Pallas kernels for 0%

commit v1 on v0

--- a/solution.py
+++ b/solution.py
@@ -6,6 +6,11 @@
 
 loss_scale = 1024.0
 f32, bf16, i32 = (jnp.float32, jnp.bfloat16, jnp.int32)
+
+
+def gather_by_exchange(shard, axis, dim):
+    copies = jnp.concatenate([shard] * lax.axis_size(axis), axis=dim)
+    return lax.all_to_all(copies, axis, dim, dim, tiled=True)
 
 
 def iota(shape, dim):
@@ -50,7 +55,7 @@
     req = dot(owner_b, jnp.where(at_slot, high, 0).astype(bf16), 1, 1) * 256.0 + dot(
         owner_b, jnp.where(at_slot, low, 0).astype(bf16), 1, 1
     )
-    q_all = lax.all_gather(query_embed[0], "group", axis=0, tiled=True)
+    q_all = gather_by_exchange(query_embed[0], "group", 0)
     got = lax.all_to_all(req, ("group", "pair"), split_axis=0, concat_axis=0, tiled=True)
     packed = got.reshape(n_group, n_pair, slots).sum(1).reshape(1, n_group * slots).astype(i32)
     pq = dot(q_all, projection, 1, 1).astype(bf16)

time: 142 us -> 149 us (1.049)
  blocking collectives: 15 us -> 0 us
  local copies, waits for them, and re-layouts: 8.09 us -> 19.1 us
  waiting for transfers between devices: 46.8 us -> 53.4 us
  starting transfers between devices: 39.6 us -> 46 us
  matrix products: 20.5 us -> 17.9 us
    all_gather x1 -> x0, blocking collectives: 15 us -> none  [shards(): q_all = lax.all_gather(query_embed[0], 'group', axis=0, tiled=True)]
    unnamed x9 -> x14, local copies, waits for them, and re-layouts: 5.06 us -> 14.7 us
    all_to_all x0 -> x1, waiting for transfers between devices: none -> 6.48 us  [gather_by_exchange(): return lax.all_to_all(copies, axis, dim, dim, tiled=True)]
    all_to_all x0 -> x1, starting transfers between devices: none -> 4.26 us  [gather_by_exchange(): return lax.all_to_all(copies, axis, dim, dim, tiled=True)]
    dot_general x17, matrix products: 20.5 us -> 17.9 us  [dot(): lax.dot_general(a, b, (((ca,), (cb,)), ((), ())), preferred_element_type=...]
    all_to_all x1, starting transfers between devices: 6.53 us -> 8.81 us  [shards(): lax.all_to_all(req, ('group', 'pair'), split_axis=0, concat_axis=0, tiled...]
  transfers between devices with their start and end apart: 7 -> 8, of which waited for: 6 -> 7; matrix products, arithmetic and copies ran while one was open for 12% -> 15% of each run, Pallas kernels for 0% -> 0%
where the time goes in v1:
time: 149 us; the launch traced here: 148 us
  waiting for transfers between devices  53.4 us (36%)
  starting transfers between devices  46 us (31%)
  local copies, waits for them, and re-layouts  19.1 us (13%)
  matrix products  17.9 us (12%)
  other arithmetic  9 us (6%)
  between operations  2.66 us (2%)
    dot_general x17, matrix products, dot(): lax.dot_general(a, b, (((ca,), (cb,)), ((), ())), preferred_element_type=...  17.9 us
    unnamed x14, local copies, waits for them, and re-layouts  14.7 us
    all_to_all x1, waiting for transfers between devices, shards(): lax.all_to_all(to_send, ('group', 'pair'), split_axis=0, concat_axis=0, t...  9.42 us
    all_to_all x1, waiting for transfers between devices, shards(): lax.all_to_all(values, ('group', 'pair'), split_axis=0, concat_axis=0, ti...  8.86 us
    all_to_all x1, starting transfers between devices, shards(): lax.all_to_all(req, ('group', 'pair'), split_axis=0, concat_axis=0, tiled...  8.81 us
    all_to_all x1, waiting for transfers between devices, shards(): lax.all_to_all(req, ('group', 'pair'), split_axis=0, concat_axis=0, tiled...  8.3 us
    all_to_all x1, waiting for transfers between devices, shards(): lax.all_to_all(u_part.T, ('group', 'pair'), split_axis=0, concat_axis=0,...  7.87 us
    all_to_all x1, starting transfers between devices, shards(): lax.all_to_all(tags, 'pair', split_axis=0, concat_axis=0, tiled=True)  7.58 us
  transfers between devices with their start and end apart: 8, of which 7 were waited for; matrix products, arithmetic and copies ran while one was open for 15% of the time, Pallas kernels for 0%

profile of v1, /device:TPU:1, one launch (start us, length us, event | category | flops | bytes accessed | tf_op | source)
XLA Modules:
  0.0 148.0 jit_solution(9280655798290494427)
XLA Ops:
  0.6 0.8 broadcast_multiply_fusion
  1.5 0.5 broadcast.374
  2.0 1.4 reduce.11
  3.5 0.3 fusion.12
  3.7 0.1 convert_element_type.121
  3.8 0.6 add.119
  4.4 7.6 %all-to-all-start = ((s32[16,1,32]{2,1,0:T(1,128)}), s32[16,1,32]{2,1,0:T(1,128)S(1)}, u32[]{:S(2)}, u32[]{:S(2)}) async-start(s32[16,1,32]{2,1,0:T(1,128)} %add.119), calls=%async_computation | async-start | bytes 16384 | tf_op jit(solution)/shard_map/all_to_all | solution.py:73
  12.0 0.7 and_multiply_fusion
  12.7 0.1 mul.135
  12.9 1.4 bitcast_dynamic-update-slice_fusion.6
  14.3 1.4 bitcast_dynamic-update-slice_fusion.5
  15.6 1.4 bitcast_dynamic-update-slice_fusion.4
  17.0 1.4 bitcast_dynamic-update-slice_fusion.3
  18.4 1.4 bitcast_dynamic-update-slice_fusion.2
  19.8 1.4 bitcast_dynamic-update-slice_fusion.1
  21.1 1.4 bitcast_dynamic-update-slice_fusion
  22.5 1.4 bitcast_dynamic-update-slice_fusion.7
  23.9 0.2 convolution_multiply_fusion.1
  24.1 0.8 convolution_add_fusion.1
  24.9 6.7 %all-to-all-start.4 = ((f32[16,1,32]{2,1,0:T(1,128)}), f32[16,1,32]{2,1,0:T(1,128)S(1)}, u32[]{:S(2)}, u32[]{:S(2)}) async-start(f32[16,1,32]{2,1,0:T(1,128)} %bitcast.79), calls=%async_computation.4 | async-start | bytes 16384 | tf_op jit(solution)/shard_map/all_to_all | solution.py:74
  31.6 0.7 reduce.12
  32.4 5.6 %all-to-all-done.4 = f32[16,1,32]{2,1,0:T(1,128)S(1)} async-done(((f32[16,1,32]{2,1,0:T(1,128)}), f32[16,1,32]{2,1,0:T(1,128)S(1)}, u32[]{:S(2)}, u32[]{:S(2)}) %all-to-all-start.4) | async-done | bytes 2080 | tf_op jit(solution)/shard_map/all_to_all | solution.py:74
  37.9 8.8 %all-to-all-start.1 = ((f32[128,1,128]{2,1,0:T(1,128)}), f32[128,1,128]{2,1,0:T(1,128)S(1)}, u32[]{:S(2)}, u32[]{:S(2)}) async-start(f32[128,1,128]{2,1,0:T(1,128)} %bitcast.3), calls=%async_computation.1 | async-start | bytes 131072 | tf_op jit(solution)/shard_map/all_to_all | solution.py:59
  46.8 0.5 broadcast.376
  47.3 0.7 reduce.13
  48.0 8.3 %all-to-all-done.1 = f32[128,1,128]{2,1,0:T(1,128)S(1)} async-done(((f32[128,1,128]{2,1,0:T(1,128)}), f32[128,1,128]{2,1,0:T(1,128)S(1)}, u32[]{:S(2)}, u32[]{:S(2)}) %all-to-all-start.1) | async-done | bytes 65568 | tf_op jit(solution)/shard_map/all_to_all | solution.py:59
  56.3 4.3 %all-to-all-start.2 = ((bf16[8,16,1024]{2,1,0:T(8,128)(2,1)}), bf16[8,16,1024]{2,1,0:T(8,128)(2,1)S(1)}, u32[]{:S(2)}, u32[]{:S(2)}) async-start(bf16[8,16,1024]{2,1,0:T(8,128)(2,1)} %bitcast.7), calls=%async_computation.2 | async-start | bytes 524288 | tf_op jit(solution)/shard_map/all_to_all | solution.py:13
  60.6 6.5 %all-to-all-done.2 = bf16[8,16,1024]{2,1,0:T(8,128)(2,1)S(1)} async-done(((bf16[8,16,1024]{2,1,0:T(8,128)(2,1)}), bf16[8,16,1024]{2,1,0:T(8,128)(2,1)S(1)}, u32[]{:S(2)}, u32[]{:S(2)}) %all-to-all-start.2) | async-done | bytes 262176 | tf_op jit(solution)/shard_map/all_to_all | solution.py:13
  67.1 0.8 convolution_convert_fusion
  67.9 3.7 %convolution_multiply_fusion = f32[128,2048]{1,0:T(8,128)S(1)} fusion(bf16[128,1024]{1,0:T(8,128)(2,1)S(1)} %convolution_convert_fusion, bf16[2048,1024]{1,0:T(8,128)(2,1)} %param.10), kind=kOutput, calls=%fused_computation.8 | convolution fusion | flops 537133056 | bytes 5505024 | tf_op jit(solution)/shard_map/dot_general | solution.py:21
  71.6 1.7 %fusion.1 = f32[128,1024]{1,0:T(8,128)S(1)} fusion(s32[1024]{0:T(1024)S(1)} %add_bitcast_fusion, f32[128,2048]{1,0:T(8,128)S(1)} %convolution_multiply_fusion), kind=kOutput, calls=%fused_computation.3 | convolution fusion | flops 540016640 | bytes 1576960 | tf_op jit(solution)/shard_map/dot_general | solution.py:21
  73.4 1.8 %fusion.9 = f32[1024]{0:T(1024)S(1)} fusion(f32[128,1024]{1,0:T(8,128)S(1)} %fusion.1, s32[1024]{0:T(1024)S(1)} %add_bitcast_fusion, f32[128,2048]{1,0:T(8,128)S(1)} %convolution_multiply_fusion, s32[1024]{0:T(1024)S(1)} %bitcast_add_fusion), kind=kOutput, calls=%fused_computation.15 | convolution fusion | flops 539753472 | bytes 1585152 | tf_op jit(solution)/shard_map/dot_general | solution.py:21
  75.2 0.6 broadcast_in_dim.47
  75.8 4.4 %all-to-all-start.3 = ((f32[128,1,128]{2,1,0:T(1,128)}), f32[128,1,128]{2,1,0:T(1,128)S(1)}, u32[]{:S(2)}, u32[]{:S(2)}) async-start(f32[128,1,128]{2,1,0:T(1,128)} %bitcast.11), calls=%async_computation.3 | async-start | bytes 131072 | tf_op jit(solution)/shard_map/all_to_all | solution.py:71
  80.2 0.2 tanh_reduce_fusion
  80.4 9.4 %all-to-all-done.3 = f32[128,1,128]{2,1,0:T(1,128)S(1)} async-done(((f32[128,1,128]{2,1,0:T(1,128)}), f32[128,1,128]{2,1,0:T(1,128)S(1)}, u32[]{:S(2)}, u32[]{:S(2)}) %all-to-all-start.3) | async-done | bytes 65568 | tf_op jit(solution)/shard_map/all_to_all | solution.py:71
  89.9 0.2 fusion.21
  90.1 0.2 fusion.11
  90.3 0.2 fusion.13
  90.5 0.6 broadcast_multiply_fusion.1
  91.1 0.3 multiply_reduce_fusion
  91.5 0.8 fusion.20
  92.3 4.5 %all-to-all-start.5 = ((f32[128,1,128]{2,1,0:T(1,128)}), f32[128,1,128]{2,1,0:T(1,128)S(1)}, u32[]{:S(2)}, u32[]{:S(2)}) async-start(f32[128,1,128]{2,1,0:T(1,128)} %bitcast.18), calls=%async_computation.5 | async-start | bytes 131072 | tf_op jit(solution)/shard_map/all_to_all | solution.py:91
  97.5 8.9 %all-to-all-done.5 = f32[128,1,128]{2,1,0:T(1,128)S(1)} async-done(((f32[128,1,128]{2,1,0:T(1,128)}), f32[128,1,128]{2,1,0:T(1,128)S(1)}, u32[]{:S(2)}, u32[]{:S(2)}) %all-to-all-start.5) | async-done | bytes 65568 | tf_op jit(solution)/shard_map/all_to_all | solution.py:91
  106.3 1.6 %fusion.6 = bf16[2048,128]{1,0:T(8,128)(2,1)S(1)} fusion(s32[1024]{0:T(1024)S(1)} %add_bitcast_fusion, bf16[16,8,8,128]{3,2,1,0:T(8,128)(2,1)S(1)} %bitcast.72, s32[1024]{0:T(1024)S(1)} %get-tuple-element.14, s32[1024]{0:T(1024)S(1)} %get-tuple-element.15, s32[128]{0:T(128)S(1)} %get-tuple-element.16, s32[128]{0:T(128)S(1)} %get-tuple-element.17, ...), kind=kOutput, calls=%fused_computation.9 | convolution fusion | flops 539754496 | bytes 800896 | tf_op jit(solution)/shard_map/dot_general | solution.py:21
  108.0 0.5 copy-done.1
  108.5 0.8 convolution_convert_fusion.1
  109.3 0.5 broadcast.377
  109.8 1.5 reduce.14
  111.2 1.8 %reshape.399 = bf16[128,2,512]{2,1,0:T(2,128)(2,1)} reshape(bf16[128,1024]{1,0:T(8,128)(2,1)} %reduce.14) | data formatting | bytes 524288
  113.1 5.6 %all-to-all-start.6 = ((bf16[128,2,512]{2,1,0:T(2,128)(2,1)}), bf16[128,2,512]{2,1,0:T(2,128)(2,1)}, u32[]{:S(2)}, u32[]{:S(2)}) async-start(bf16[128,2,512]{2,1,0:T(2,128)(2,1)} %reshape.399), calls=%async_computation.6 | async-start | bytes 524288 | tf_op jit(solution)/shard_map/all_to_all | solution.py:100
  118.7 0.8 copy.20
  119.5 3.3 %multiply_convert_fusion = bf16[2048,1024]{1,0:T(8,128)(2,1)} fusion(bf16[2048,128]{1,0:T(8,128)(2,1)S(1)} %fusion.6, bf16[128,1024]{1,0:T(8,128)(2,1)S(1)} %convolution_convert_fusion), kind=kOutput, calls=%fused_computation | convolution fusion | flops 541065216 | bytes 4980736 | tf_op jit(solution)/shard_map/dot_general | solution.py:21
  122.8 7.0 %all-to-all-done.6 = bf16[128,2,512]{2,1,0:T(2,128)(2,1)} async-done(((bf16[128,2,512]{2,1,0:T(2,128)(2,1)}), bf16[128,2,512]{2,1,0:T(2,128)(2,1)}, u32[]{:S(2)}, u32[]{:S(2)}) %all-to-all-start.6) | async-done | bytes 262176 | tf_op jit(solution)/shard_map/all_to_all | solution.py:100
  129.7 4.2 %all-to-all-start.7 = ((bf16[128,8,128]{2,1,0:T(8,128)(2,1)}), bf16[128,8,128]{2,1,0:T(8,128)(2,1)S(1)}, u32[]{:S(2)}, u32[]{:S(2)}) async-start(bf16[128,8,128]{2,1,0:T(8,128)(2,1)} %bitcast.25), calls=%async_computation.7 | async-start | bytes 524288 | tf_op jit(solution)/shard_map/all_to_all | solution.py:101
  133.9 2.2 %reshape.400 = bf16[128,1,1024]{2,1,0:T(2,128)(2,1)S(1)} reshape(bf16[128,2,512]{2,1,0:T(2,128)(2,1)} %all-to-all-done.6) | data formatting | bytes 524288
  136.1 0.5 convert_reduce_fusion.1
  136.6 0.4 fusion.65
  137.0 0.4 fusion.64
  137.4 7.9 %all-to-all-done.7 = bf16[128,8,128]{2,1,0:T(8,128)(2,1)S(1)} async-done(((bf16[128,8,128]{2,1,0:T(8,128)(2,1)}), bf16[128,8,128]{2,1,0:T(8,128)(2,1)S(1)}, u32[]{:S(2)}, u32[]{:S(2)}) %all-to-all-start.7) | async-done | bytes 262176 | tf_op jit(solution)/shard_map/all_to_all | solution.py:101
  145.3 0.1 convert_reduce_fusion
  145.4 0.1 fusion.48
  145.5 0.8 convolution_add_fusion.2
  146.3 0.6 add.131
  (23 shorter events, 0.5 us)
Async XLA Ops:
  0.6 66.5 %copy-start = (bf16[1024,1024]{1,0:T(8,128)(2,1)S(1)}, bf16[1024,1024]{1,0:T(8,128)(2,1)}, u32[]{:S(2)}) copy-start(bf16[1024,1024]{1,0:T(8,128)(2,1)} %param.11) | copy-start | bytes 6291460
  4.4 20.5 %all-to-all-start = ((s32[16,1,32]{2,1,0:T(1,128)}), s32[16,1,32]{2,1,0:T(1,128)S(1)}, u32[]{:S(2)}, u32[]{:S(2)}) async-start(s32[16,1,32]{2,1,0:T(1,128)} %add.119), calls=%async_computation | async-start | bytes 16384 | tf_op jit(solution)/shard_map/all_to_all | solution.py:73
  24.9 13.0 %all-to-all-start.4 = ((f32[16,1,32]{2,1,0:T(1,128)}), f32[16,1,32]{2,1,0:T(1,128)S(1)}, u32[]{:S(2)}, u32[]{:S(2)}) async-start(f32[16,1,32]{2,1,0:T(1,128)} %bitcast.79), calls=%async_computation.4 | async-start | bytes 16384 | tf_op jit(solution)/shard_map/all_to_all | solution.py:74
  37.9 18.4 %all-to-all-start.1 = ((f32[128,1,128]{2,1,0:T(1,128)}), f32[128,1,128]{2,1,0:T(1,128)S(1)}, u32[]{:S(2)}, u32[]{:S(2)}) async-start(f32[128,1,128]{2,1,0:T(1,128)} %bitcast.3), calls=%async_computation.1 | async-start | bytes 131072 | tf_op jit(solution)/shard_map/all_to_all | solution.py:59
  56.3 10.8 %all-to-all-start.2 = ((bf16[8,16,1024]{2,1,0:T(8,128)(2,1)}), bf16[8,16,1024]{2,1,0:T(8,128)(2,1)S(1)}, u32[]{:S(2)}, u32[]{:S(2)}) async-start(bf16[8,16,1024]{2,1,0:T(8,128)(2,1)} %bitcast.7), calls=%async_computation.2 | async-start | bytes 524288 | tf_op jit(solution)/shard_map/all_to_all | solution.py:13
  75.8 14.1 %all-to-all-start.3 = ((f32[128,1,128]{2,1,0:T(1,128)}), f32[128,1,128]{2,1,0:T(1,128)S(1)}, u32[]{:S(2)}, u32[]{:S(2)}) async-start(f32[128,1,128]{2,1,0:T(1,128)} %bitcast.11), calls=%async_computation.3 | async-start | bytes 131072 | tf_op jit(solution)/shard_map/all_to_all | solution.py:71
  92.3 14.0 %all-to-all-start.5 = ((f32[128,1,128]{2,1,0:T(1,128)}), f32[128,1,128]{2,1,0:T(1,128)S(1)}, u32[]{:S(2)}, u32[]{:S(2)}) async-start(f32[128,1,128]{2,1,0:T(1,128)} %bitcast.18), calls=%async_computation.5 | async-start | bytes 131072 | tf_op jit(solution)/shard_map/all_to_all | solution.py:91
  106.3 2.2 %copy-start.1 = (bf16[2048,1024]{1,0:T(8,128)(2,1)S(1)}, bf16[2048,1024]{1,0:T(8,128)(2,1)}, u32[]{:S(2)}) copy-start(bf16[2048,1024]{1,0:T(8,128)(2,1)} %param.10) | copy-start | bytes 12582916
  113.1 16.7 %all-to-all-start.6 = ((bf16[128,2,512]{2,1,0:T(2,128)(2,1)}), bf16[128,2,512]{2,1,0:T(2,128)(2,1)}, u32[]{:S(2)}, u32[]{:S(2)}) async-start(bf16[128,2,512]{2,1,0:T(2,128)(2,1)} %reshape.399), calls=%async_computation.6 | async-start | bytes 524288 | tf_op jit(solution)/shard_map/all_to_all | solution.py:100
  129.7 15.5 %all-to-all-start.7 = ((bf16[128,8,128]{2,1,0:T(8,128)(2,1)}), bf16[128,8,128]{2,1,0:T(8,128)(2,1)S(1)}, u32[]{:S(2)}, u32[]{:S(2)}) async-start(bf16[128,8,128]{2,1,0:T(8,128)(2,1)} %bitcast.25), calls=%async_computation.7 | async-start | bytes 524288 | tf_op jit(solution)/shard_map/all_to_all | solution.py:101
